TPU v7x, 32 devices: a whole 2x2x4 slice. The times are simulated.
32 devices in a mesh: rows: 8 (over z, x), chan: 4 (over y, core).
Axes of the slice: x: 2, y: 2, z: 4, core: 2. Of those that a mesh axis runs over, the one named last changes fastest.
Arguments:
- frames: bfloat16 [9, 32, 480, 256], P(None, 'rows', 'chan'), may hold values from -450 to 450
- spatial_weight: bfloat16 [256, 2304], P('rows'), may hold values from -0.125 to 0.125
- temporal_weight: bfloat16 [256, 768], P('rows'), may hold values from -0.21875 to 0.21875
- down_weight: bfloat16 [256, 2304], P('rows'), may hold values from -0.125 to 0.125
- norm_gain: float32 [256], replicated, may hold values from 0.5 to 1.5
- norm_shift: float32 [256], replicated, may hold values from -3 to 3
- down_bias: float32 [256], replicated, may hold values from -3 to 3
Outputs:
- latent: bfloat16 [9, 16, 240, 256], P(None, 'rows', 'chan')
All inputs are finite; a program needn't handle non-finite values.
Results may differ from a plain program's by a relative error of at most 0.0053.
Values may be sent and summed in bfloat16 or wider, within the bound.
No kernel may reach another device: no remote copies, remote signals or barrier semaphores. Data moves between devices by JAX's collectives and lax.ppermute only.
A program may use at most 128 MiB of HBM per device.

v0:
```python
import jax
import jax.numpy as jnp
from jax import lax
from jax.sharding import PartitionSpec as P

GROUPS = 32
epsilon = 1e-06


def extended_2(cells, sides, width):
    for axis, dim in sides:
        count = lax.axis_size(axis)
        ends = count - 1
        head = lax.slice_in_dim(cells, 0, width, axis=dim)
        tail = lax.slice_in_dim(cells, cells.shape[dim] - width, cells.shape[dim], axis=dim)
        cells = jnp.concatenate(
            [
                lax.ppermute(tail, axis, [(i, (i + 1) % count) for i in range(ends)]),
                cells,
                lax.ppermute(head, axis, [((i + 1) % count, i) for i in range(ends)]),
            ],
            axis=dim,
        )
    return cells


def passed_along(block, axis, distance):
    devices = range(lax.axis_size(axis))
    route = [(i - distance, i) for i in devices if i - distance in devices]
    return lax.ppermute(block, axis, route)


def spatial_taps(padded, weight_rows, width_out):
    rows_out = padded.shape[1] - 2
    cols_out = padded.shape[2] - 2
    summed = None
    for tap_index in range(9):
        row_offset = tap_index // 3
        col_offset = tap_index % 3
        window = padded[
            :, row_offset : row_offset + rows_out, col_offset : col_offset + cols_out, :
        ]
        weight_panel = weight_rows[:, tap_index * width_out : (tap_index + 1) * width_out]
        product = jnp.einsum(
            "fijc,co->fijo", window, weight_panel, preferred_element_type=jnp.float32
        )
        summed = product if summed is None else summed + product
    return summed


def temporal_taps(values, weight_rows, width_out):
    frame_count = values.shape[0]
    summed = None
    for tap_index in range(3):
        lag_frames = 2 - tap_index
        if lag_frames > 0:
            delayed = jnp.concatenate(
                [jnp.repeat(values[:1], lag_frames, axis=0), values[: frame_count - lag_frames]],
                axis=0,
            )
        else:
            delayed = values
        weight_panel = weight_rows[:, tap_index * width_out : (tap_index + 1) * width_out]
        product = jnp.einsum(
            "fijc,co->fijo", delayed, weight_panel, preferred_element_type=jnp.float32
        )
        summed = product if summed is None else summed + product
    return summed


def down_taps(extended, weight_rows, width_out):
    rows_out = (extended.shape[1] - 1) // 2
    cols_out = (extended.shape[2] - 1) // 2
    summed = None
    for tap_index in range(9):
        row_offset = tap_index // 3
        col_offset = tap_index % 3
        window = extended[
            :,
            row_offset : row_offset + 2 * rows_out : 2,
            col_offset : col_offset + 2 * cols_out : 2,
            :,
        ]
        weight_panel = weight_rows[:, tap_index * width_out : (tap_index + 1) * width_out]
        product = jnp.einsum(
            "fijc,co->fijo", window, weight_panel, preferred_element_type=jnp.float32
        )
        summed = product if summed is None else summed + product
    return summed


def group_reduce(partial_sums):
    return lax.psum(partial_sums, ("rows", "chan"))


def place_groups(channel_sums, group_width):
    local_sums = channel_sums.reshape(-1, group_width).sum(axis=1)
    return local_sums


def channel_values(group_vector, group_width):
    return jnp.repeat(group_vector, group_width)


def per_device(
    frames, spatial_weight, temporal_weight, down_weight, norm_gain, norm_shift, down_bias
):
    full_spatial, full_temporal, full_down = (
        lax.all_gather(spatial_weight, "rows", axis=0, tiled=True),
        lax.all_gather(temporal_weight, "rows", axis=0, tiled=True),
        lax.all_gather(down_weight, "rows", axis=0, tiled=True),
    )
    channels = full_spatial.shape[0]
    group_width = channels // GROUPS
    frame_count = frames.shape[0]
    rows_dev = frames.shape[1]
    width_all = frames.shape[2] * lax.axis_size("chan")
    cell_count = float(frame_count * rows_dev * lax.axis_size("rows") * width_all * group_width)
    padded = extended_2(frames, (("rows", 1), ("chan", 2)), 1)
    first = spatial_taps(padded, full_spatial, channels).astype(jnp.bfloat16)
    hidden = temporal_taps(first, full_temporal, channels)
    channel_sums = jnp.sum(hidden, axis=(0, 1, 2))
    totals = group_reduce(place_groups(channel_sums, group_width)[None])
    means = totals[0] / cell_count
    chan_mean = channel_values(means, group_width)
    centered = hidden - chan_mean
    spread = group_reduce(
        place_groups(jnp.sum(centered * centered, axis=(0, 1, 2)), group_width)[None]
    )
    variance = spread[0] / cell_count
    chan_var = channel_values(variance, group_width)
    act = jax.nn.silu(centered * lax.rsqrt(chan_var + epsilon) * norm_gain + norm_shift).astype(
        jnp.bfloat16
    )
    below = passed_along(act[:, :1], "rows", -1)
    extended = jnp.concatenate([act, below], axis=1)
    beside = passed_along(extended[:, :, :1], "chan", -1)
    extended = jnp.concatenate([extended, beside], axis=2)
    latent = down_taps(extended, full_down, channels) + down_bias
    return latent.astype(jnp.bfloat16)


def solution(mesh):
    placed = (
        P(None, "rows", "chan", None),
        P("rows", None),
        P("rows", None),
        P("rows", None),
        P(),
        P(),
        P(),
    )
    return jax.shard_map(
        per_device,
        mesh=mesh,
        in_specs=placed,
        out_specs=P(None, "rows", "chan", None),
        check_vma=False,
    )
```

profile of v0, /device:TPU:3, one launch (start us, length us, event | category | flops | bytes accessed | tf_op | source)
XLA Modules:
  0.0 319.5 jit_solution(4577024968184721207)
XLA Ops:
  7.3 2.1 fusion.64
  9.4 3.2 collective-permute-start
  12.6 2.9 collective-permute-start.1
  15.5 22.7 %collective-permute-done = bf16[9,1,120,256]{3,2,1,0:T(8,128)(2,1)} collective-permute-done((bf16[9,1,120,256]{3,2,1,0:T(8,128)(2,1)S(1)}, bf16[9,1,120,256]{3,2,1,0:T(8,128)(2,1)}, u32[]{:S(2)}, u32[]{:S(2)}) %collective-permute-start) | collective-permute-done | bytes 552992 | tf_op jit(solution)/shard_map/ppermute | solution.py:18
  38.2 1.1 constant_dynamic-update-slice_fusion.2
  39.3 1.8 constant_dynamic-update-slice_fusion.1
  41.1 1.1 constant_dynamic-update-slice_fusion
  42.3 4.6 %collective-permute-start.2 = (bf16[9,6,1,256]{3,2,1,0:T(2,128)(2,1)S(1)}, bf16[9,6,1,256]{3,2,1,0:T(2,128)(2,1)S(1)}, u32[]{:S(2)}, u32[]{:S(2)}) collective-permute-start(bf16[9,6,1,256]{3,2,1,0:T(2,128)(2,1)S(1)} %get-tuple-element.6), channel_id=1, source_target_pairs={{0,1},{1,2},{2,3},{4,5},{5,6},{6,7},{8,9},{9,10},{10,11},{12,13},{... | collective-permute-start | bytes 82952 | tf_op jit(solution)/shard_map/ppermute | solution.py:18
  46.9 25.9 %all_gather.10 = bf16[256,768]{1,0:T(8,128)(2,1)} all-gather(bf16[32,768]{1,0:T(8,128)(2,1)S(1)} %copy-done.12), channel_id=1, replica_groups=mesh['rows'=8,'chan'=4] {'rows'}, dimensions={0}, use_global_device_ids=true | all-gather | bytes 442368 | tf_op jit(solution)/shard_map/all_gather | solution.py:110
  72.8 5.5 %collective-permute-start.3 = (bf16[9,6,1,256]{3,2,1,0:T(2,128)(2,1)S(1)}, bf16[9,6,1,256]{3,2,1,0:T(2,128)(2,1)S(1)}, u32[]{:S(2)}, u32[]{:S(2)}) collective-permute-start(bf16[9,6,1,256]{3,2,1,0:T(2,128)(2,1)S(1)} %get-tuple-element.5), channel_id=1, source_target_pairs={{1,0},{2,1},{3,2},{5,4},{6,5},{7,6},{9,8},{10,9},{11,10},{13,12},{... | collective-permute-start | bytes 82952 | tf_op jit(solution)/shard_map/ppermute | solution.py:20
  78.4 3.8 %fusion.15 = f32[9,4,120,256]{3,2,1,0:T(8,128)} fusion(bf16[9,6,120,256]{3,2,1,0:T(8,128)(2,1)S(1)} %constant_dynamic-update-slice_fusion, bf16[9,6,1,256]{3,2,1,0:T(2,128)(2,1)S(1)} %collective-permute-done.2, bf16[256,2304]{1,0:T(8,128)(2,1)} %all-gather.3.cloned.1.call-done), kind=kOutput, calls=%fused_computation.29 | convolution fusion | flops 570654720 | bytes 7900160 | tf_op jit(solution)/shard_map/fijc,co->fijo/dot_general | solution.py:44
  82.2 2.9 fusion.18
  85.1 2.8 fusion.12
  87.8 2.9 fusion.9
  90.8 2.9 fusion.22
  93.6 3.9 %fusion = f32[9,4,120,256]{3,2,1,0:T(8,128)} fusion(bf16[9,4,120,256]{3,2,1,0:T(8,128)(2,1)S(1)} %copy-done, bf16[9,1,120,256]{3,2,1,0:T(8,128)(2,1)} %collective-permute-done, bf16[256,2304]{1,0:T(8,128)(2,1)S(1)} %copy-done.11), kind=kOutput, calls=%fused_computation.15 | convolution fusion | flops 571760640 | bytes 7319552 | tf_op jit(solution)/shard_map/fijc,co->fijo/dot_general | solution.py:44
  97.5 1.8 fusion.4
  99.3 2.9 fusion.50
  102.2 12.6 %add_convert_fusion = bf16[9,4,120,256]{3,2,1,0:T(8,128)(2,1)} fusion(f32[9,4,120,256]{3,2,1,0:T(8,128)S(1)} %fusion.4, f32[9,4,120,256]{3,2,1,0:T(8,128)} %fusion.22, f32[9,4,120,256]{3,2,1,0:T(8,128)} %fusion.9, f32[9,4,120,256]{3,2,1,0:T(8,128)} %fusion.50, f32[9,4,120,256]{3,2,1,0:T(8,128)} %fusion.15, f32[9,4,120,256]{3,2,1,0:T(8,128)} %fusion.12, ...), kind=kOutput, calls=%fused_computation.7 | convolution fusion | flops 580608000 | bytes 41105408 | tf_op jit(solution)/shard_map/fijc,co->fijo/dot_general | solution.py:44
  114.8 1.6 copy-done.1
  120.4 3.0 fusion.65
  123.7 38.6 %psum.14 = f32[1,32]{1,0:T(1,128)S(1)} all-reduce(f32[1,32]{1,0:T(1,128)S(1)} %bitcast.127), channel_id=1, replica_groups=mesh['rows'=8,'chan'=4] {'rows','chan'}, use_global_device_ids=true, to_apply=%region_2.0 | all-reduce | flops 32 | bytes 256 | tf_op jit(solution)/shard_map/psum | solution.py:93
  162.5 2.9 multiply_reduce_fusion
  165.5 41.8 %psum.15 = f32[1,32]{1,0:T(1,128)S(1)} all-reduce(f32[1,32]{1,0:T(1,128)S(1)} %bitcast.126), channel_id=1, replica_groups=mesh['rows'=8,'chan'=4] {'rows','chan'}, use_global_device_ids=true, to_apply=%region_5.0 | all-reduce | flops 32 | bytes 256 | tf_op jit(solution)/shard_map/psum | solution.py:93
  207.5 3.6 %multiply_convert_fusion = bf16[9,4,120,256]{3,2,1,0:T(8,128)(2,1)S(1)} fusion(f32[9,4,120,256]{3,2,1,0:T(8,128)} %get-tuple-element.12, f32[256]{0:T(256)S(1)} %copy-done.13, f32[256]{0:T(256)S(1)} %copy-done.14, f32[256]{0:T(256)S(1)} %rsqrt.16, f32[256]{0:T(256)S(1)} %sub.10), kind=kLoop, calls=%fused_computation.4 | loop fusion | flops 9953280 | bytes 6639616 | tf_op jit(solution)/shard_map/convert_element_type | solution.py:132
  212.0 1.9 collective-permute-start.4
  214.8 2.2 fusion.48
  217.1 10.4 %collective-permute-done.4 = bf16[9,1,120,256]{3,2,1,0:T(8,128)(2,1)S(1)} collective-permute-done((bf16[9,1,120,256]{3,2,1,0:T(8,128)(2,1)}, bf16[9,1,120,256]{3,2,1,0:T(8,128)(2,1)S(1)}, u32[]{:S(2)}, u32[]{:S(2)}) %collective-permute-start.4) | collective-permute-done | bytes 552992 | tf_op jit(solution)/shard_map/ppermute | solution.py:30
  227.5 1.8 pad_maximum_fusion
  229.3 10.3 %slice.188 = bf16[9,2,60,256]{3,2,1,0:T(8,128)(2,1)} slice(bf16[9,5,120,256]{3,2,1,0:T(8,128)(2,1)} %pad_maximum_fusion), slice={[0:9:1], [1:5:2], [0:120:2], [0:256:1]} | slice | bytes 1105920 | tf_op jit(solution)/shard_map/slice | solution.py:78
  239.6 8.5 %slice.194 = bf16[9,2,60,256]{3,2,1,0:T(8,128)(2,1)S(1)} slice(bf16[9,5,120,256]{3,2,1,0:T(8,128)(2,1)} %pad_maximum_fusion), slice={[0:9:1], [2:5:2], [0:120:2], [0:256:1]} | slice | bytes 1105920 | tf_op jit(solution)/shard_map/slice | solution.py:78
  248.2 4.5 %collective-permute-start.5 = (bf16[9,5,1,256]{3,2,1,0:T(2,128)(2,1)S(1)}, bf16[9,5,1,256]{3,2,1,0:T(2,128)(2,1)S(1)}, u32[]{:S(2)}, u32[]{:S(2)}) collective-permute-start(bf16[9,5,1,256]{3,2,1,0:T(2,128)(2,1)S(1)} %fusion.51), channel_id=1, source_target_pairs={{1,0},{2,1},{3,2},{5,4},{6,5},{7,6},{9,8},{10,9},{11,10},{13,12},{... | collective-permute-start | bytes 69128 | tf_op jit(solution)/shard_map/ppermute | solution.py:30
  252.7 2.3 fusion.47
  254.9 2.2 fusion.44
  257.2 2.0 pad_maximum_fusion.1
  259.2 10.5 %slice.184 = bf16[9,2,60,256]{3,2,1,0:T(8,128)(2,1)} slice(bf16[9,5,121,256]{3,2,1,0:T(8,128)(2,1)} %pad_maximum_fusion.1), slice={[0:9:1], [0:4:2], [1:121:2], [0:256:1]} | slice | bytes 1105920 | tf_op jit(solution)/shard_map/slice | solution.py:78
  269.6 10.2 %slice.198 = bf16[9,2,60,256]{3,2,1,0:T(8,128)(2,1)} slice(bf16[9,5,121,256]{3,2,1,0:T(8,128)(2,1)} %pad_maximum_fusion.1), slice={[0:9:1], [2:5:2], [2:121:2], [0:256:1]} | slice | bytes 1105920 | tf_op jit(solution)/shard_map/slice | solution.py:78
  279.8 10.1 %slice.196 = bf16[9,2,60,256]{3,2,1,0:T(8,128)(2,1)} slice(bf16[9,5,121,256]{3,2,1,0:T(8,128)(2,1)} %pad_maximum_fusion.1), slice={[0:9:1], [2:5:2], [1:121:2], [0:256:1]} | slice | bytes 1105920 | tf_op jit(solution)/shard_map/slice | solution.py:78
  289.9 6.0 %slice.192 = bf16[9,2,60,256]{3,2,1,0:T(8,128)(2,1)} slice(bf16[9,5,121,256]{3,2,1,0:T(8,128)(2,1)S(1)} %copy-done.2), slice={[0:9:1], [1:5:2], [2:121:2], [0:256:1]} | slice | bytes 1105920 | tf_op jit(solution)/shard_map/slice | solution.py:78
  295.9 5.9 %slice.190 = bf16[9,2,60,256]{3,2,1,0:T(8,128)(2,1)} slice(bf16[9,5,121,256]{3,2,1,0:T(8,128)(2,1)S(1)} %copy-done.2), slice={[0:9:1], [1:5:2], [1:121:2], [0:256:1]} | slice | bytes 1105920 | tf_op jit(solution)/shard_map/slice | solution.py:78
  301.8 1.0 slice.186
  302.8 1.5 fusion.42
  304.3 1.5 fusion.43
  305.9 1.2 fusion.45
  307.1 1.4 fusion.46
  308.5 1.2 convolution_add_fusion.1
  309.8 1.5 fusion.41
  311.3 1.4 copy.9
  (63 shorter events, 7.4 us)
Async XLA Ops:
  6.5 71.8 %all-gather.3.cloned.1.call-start = ((), (), s32[]{:S(2)}) async-start(), calls=%async_computation | async-start | bytes 1327104 | tf_op jit(solution)/shard_map/all_gather | solution.py:109
  7.3 207.6 %all-gather.5.cloned.1.call-start = ((), (), s32[]{:S(2)}) async-start(), calls=%async_computation.1 | async-start | bytes 1327104 | tf_op jit(solution)/shard_map/all_gather | solution.py:111
  9.4 28.8 %collective-permute-start = (bf16[9,1,120,256]{3,2,1,0:T(8,128)(2,1)S(1)}, bf16[9,1,120,256]{3,2,1,0:T(8,128)(2,1)}, u32[]{:S(2)}, u32[]{:S(2)}) collective-permute-start(bf16[9,1,120,256]{3,2,1,0:T(8,128)(2,1)S(1)} %get-tuple-element.9), channel_id=1, source_target_pairs={{0,4},{4,8},{8,12},{12,16},{16,20},{20,24},{24,28},{1,5},{5,9},{9,... | collective-permute-start | bytes 1658888 | tf_op jit(solution)/shard_map/ppermute | solution.py:18
  12.6 28.5 %collective-permute-start.1 = (bf16[9,1,120,256]{3,2,1,0:T(8,128)(2,1)}, bf16[9,1,120,256]{3,2,1,0:T(8,128)(2,1)}, u32[]{:S(2)}, u32[]{:S(2)}) collective-permute-start(bf16[9,1,120,256]{3,2,1,0:T(8,128)(2,1)} %get-tuple-element.10), channel_id=1, source_target_pairs={{4,0},{8,4},{12,8},{16,12},{20,16},{24,20},{28,24},{5,1},{9,5},{13... | collective-permute-start | bytes 1658888 | tf_op jit(solution)/shard_map/ppermute | solution.py:20
  39.3 7.6 %copy-start.12 = (bf16[32,768]{1,0:T(8,128)(2,1)S(1)}, bf16[32,768]{1,0:T(8,128)(2,1)}, u32[]{:S(2)}) copy-start(bf16[32,768]{1,0:T(8,128)(2,1)} %param.9) | copy-start | bytes 147460
  42.3 36.0 %collective-permute-start.2 = (bf16[9,6,1,256]{3,2,1,0:T(2,128)(2,1)S(1)}, bf16[9,6,1,256]{3,2,1,0:T(2,128)(2,1)S(1)}, u32[]{:S(2)}, u32[]{:S(2)}) collective-permute-start(bf16[9,6,1,256]{3,2,1,0:T(2,128)(2,1)S(1)} %get-tuple-element.6), channel_id=1, source_target_pairs={{0,1},{1,2},{2,3},{4,5},{5,6},{6,7},{8,9},{9,10},{10,11},{12,13},{... | collective-permute-start | bytes 82952 | tf_op jit(solution)/shard_map/ppermute | solution.py:18
  72.8 12.3 %collective-permute-start.3 = (bf16[9,6,1,256]{3,2,1,0:T(2,128)(2,1)S(1)}, bf16[9,6,1,256]{3,2,1,0:T(2,128)(2,1)S(1)}, u32[]{:S(2)}, u32[]{:S(2)}) collective-permute-start(bf16[9,6,1,256]{3,2,1,0:T(2,128)(2,1)S(1)} %get-tuple-element.5), channel_id=1, source_target_pairs={{1,0},{2,1},{3,2},{5,4},{6,5},{7,6},{9,8},{10,9},{11,10},{13,12},{... | collective-permute-start | bytes 82952 | tf_op jit(solution)/shard_map/ppermute | solution.py:20
  78.4 3.8 %copy-start.11 = (bf16[256,2304]{1,0:T(8,128)(2,1)S(1)}, bf16[256,2304]{1,0:T(8,128)(2,1)}, u32[]{:S(2)}) copy-start(bf16[256,2304]{1,0:T(8,128)(2,1)} %all-gather.3.cloned.1.call-done) | copy-start | bytes 3538948
  90.8 2.9 copy-start
  114.8 1.6 copy-start.1
  116.4 1.0 copy-start.10
  117.4 1.5 slice-start
  118.9 1.5 slice-start.1
  123.5 84.1 %copy-start.13 = (f32[256]{0:T(256)S(1)}, f32[256]{0:T(256)}, u32[]{:S(2)}) copy-start(f32[256]{0:T(256)} %param.12) | copy-start | bytes 3076
  123.5 84.1 %copy-start.14 = (f32[256]{0:T(256)S(1)}, f32[256]{0:T(256)}, u32[]{:S(2)}) copy-start(f32[256]{0:T(256)} %param.11) | copy-start | bytes 3076
  212.0 15.5 %collective-permute-start.4 = (bf16[9,1,120,256]{3,2,1,0:T(8,128)(2,1)}, bf16[9,1,120,256]{3,2,1,0:T(8,128)(2,1)S(1)}, u32[]{:S(2)}, u32[]{:S(2)}) collective-permute-start(bf16[9,1,120,256]{3,2,1,0:T(8,128)(2,1)} %slice.226), channel_id=1, source_target_pairs={{4,0},{8,4},{12,8},{16,12},{20,16},{24,20},{28,24},{5,1},{9,5},{13... | collective-permute-start | bytes 1658888 | tf_op jit(solution)/shard_map/ppermute | solution.py:30
  248.1 4.6 %copy-start.8 = (bf16[9,2,60,256]{3,2,1,0:T(8,128)(2,1)S(1)}, bf16[9,2,60,256]{3,2,1,0:T(8,128)(2,1)}, u32[]{:S(2)}) copy-start(bf16[9,2,60,256]{3,2,1,0:T(8,128)(2,1)} %slice.188) | copy-start | bytes 1658884
  248.2 9.0 %collective-permute-start.5 = (bf16[9,5,1,256]{3,2,1,0:T(2,128)(2,1)S(1)}, bf16[9,5,1,256]{3,2,1,0:T(2,128)(2,1)S(1)}, u32[]{:S(2)}, u32[]{:S(2)}) collective-permute-start(bf16[9,5,1,256]{3,2,1,0:T(2,128)(2,1)S(1)} %fusion.51), channel_id=1, source_target_pairs={{1,0},{2,1},{3,2},{5,4},{6,5},{7,6},{9,8},{10,9},{11,10},{13,12},{... | collective-permute-start | bytes 69128 | tf_op jit(solution)/shard_map/ppermute | solution.py:30
  259.2 30.7 %copy-start.2 = (bf16[9,5,121,256]{3,2,1,0:T(8,128)(2,1)S(1)}, bf16[9,5,121,256]{3,2,1,0:T(8,128)(2,1)}, u32[]{:S(2)}) copy-start(bf16[9,5,121,256]{3,2,1,0:T(8,128)(2,1)} %pad_maximum_fusion.1) | copy-start | bytes 8363524
  302.8 3.1 copy-start.9
  302.8 4.3 %copy-start.7 = (bf16[9,2,60,256]{3,2,1,0:T(8,128)(2,1)S(1)}, bf16[9,2,60,256]{3,2,1,0:T(8,128)(2,1)}, u32[]{:S(2)}) copy-start(bf16[9,2,60,256]{3,2,1,0:T(8,128)(2,1)} %slice.190) | copy-start | bytes 1658884
  304.3 4.2 %copy-start.5 = (f32[9,2,60,256]{3,2,1,0:T(8,128)S(1)}, f32[9,2,60,256]{3,2,1,0:T(8,128)}, u32[]{:S(2)}) copy-start(f32[9,2,60,256]{3,2,1,0:T(8,128)} %fusion.48) | copy-start | bytes 3317764
  304.3 4.2 %copy-start.6 = (bf16[9,2,60,256]{3,2,1,0:T(8,128)(2,1)S(1)}, bf16[9,2,60,256]{3,2,1,0:T(8,128)(2,1)}, u32[]{:S(2)}) copy-start(bf16[9,2,60,256]{3,2,1,0:T(8,128)(2,1)} %slice.184) | copy-start | bytes 1658884
  307.1 2.6 copy-start.3
  307.1 2.6 copy-start.4
  307.1 2.6 copy-start.15
Sparse Core Ops, SparseCore 0:
  9.5 52.3 all-gather.2
  64.2 39.7 all-gather.4
where the time goes:
time: 322 us; the launch traced here: 320 us
  blocking collectives  106 us (33%)
  local copies, waits for them, and re-layouts  76.4 us (24%)
  matrix products  56 us (17%)
  waiting for transfers between devices  33.9 us (11%)
  starting transfers between devices  22.6 us (7%)
  between operations  13.8 us (4%)
  other arithmetic  10.5 us (3%)
    psum x2, blocking collectives, group_reduce(): return lax.psum(partial_sums, ('rows', 'chan'))  80.4 us
    slice x9, local copies, waits for them, and re-layouts, down_taps(): extended[:, row_offset:row_offset + 2 * rows_out:2, col_offset:col_offset...  63.3 us
    dot_general x9, matrix products, spatial_taps(): jnp.einsum('fijc,co->fijo', window, weight_panel, preferred_element_type=...  36.4 us
    all_gather x1, blocking collectives, per_device(): lax.all_gather(temporal_weight, 'rows', axis=0, tiled=True)  25.9 us
    ppermute x2, waiting for transfers between devices, extended_2(): lax.ppermute(tail, axis, [(i, (i + 1) % count) for i in range(ends)])  22.7 us
    dot_general x9, matrix products, down_taps(): jnp.einsum('fijc,co->fijo', window, weight_panel, preferred_element_type=...  15.1 us
    ppermute x2, waiting for transfers between devices, passed_along(): return lax.ppermute(block, axis, route)  10.4 us
    ppermute x2, starting transfers between devices, extended_2(): lax.ppermute(head, axis, [((i + 1) % count, i) for i in range(ends)])  8.43 us
  transfers between devices with their start and end apart: 8, of which 2 were waited for; matrix products, arithmetic and copies ran while one was open for 20% of the time, Pallas kernels for 0%

commit v1 on v0

--- a/solution.py
+++ b/solution.py
@@ -90,7 +90,7 @@
 
 
 def group_reduce(partial_sums):
-    return lax.psum(partial_sums, ("rows", "chan"))
+    return jnp.sum(lax.all_gather(partial_sums, axis_name=("rows", "chan")), 0)
 
 
 def place_groups(channel_sums, group_width):

time: 322 us -> 322 us (level)
    psum x2 -> x0, blocking collectives: 80.4 us -> none  [group_reduce(): return lax.psum(partial_sums, ('rows', 'chan'))]
    unnamed x0 -> x2, blocking collectives: none -> 80.4 us
where the time goes in v1:
time: 322 us; the launch traced here: 320 us
  blocking collectives  106 us (33%)
  local copies, waits for them, and re-layouts  77 us (24%)
  matrix products  55.8 us (17%)
  waiting for transfers between devices  33.9 us (11%)
  starting transfers between devices  22.6 us (7%)
  between operations  13.8 us (4%)
  other arithmetic  10.6 us (3%)
    unnamed x2, blocking collectives  80.4 us
    slice x9, local copies, waits for them, and re-layouts, down_taps(): extended[:, row_offset:row_offset + 2 * rows_out:2, col_offset:col_offset...  63.3 us
    dot_general x9, matrix products, spatial_taps(): jnp.einsum('fijc,co->fijo', window, weight_panel, preferred_element_type=...  36.3 us
    all_gather x1, blocking collectives, per_device(): lax.all_gather(temporal_weight, 'rows', axis=0, tiled=True)  25.9 us
    ppermute x2, waiting for transfers between devices, extended_2(): lax.ppermute(tail, axis, [(i, (i + 1) % count) for i in range(ends)])  22.7 us
    dot_general x9, matrix products, down_taps(): jnp.einsum('fijc,co->fijo', window, weight_panel, preferred_element_type=...  15 us
    ppermute x2, waiting for transfers between devices, passed_along(): return lax.ppermute(block, axis, route)  10.4 us
    ppermute x2, starting transfers between devices, extended_2(): lax.ppermute(head, axis, [((i + 1) % count, i) for i in range(ends)])  8.43 us
  transfers between devices with their start and end apart: 8, of which 2 were waited for; matrix products, arithmetic and copies ran while one was open for 20% of the time, Pallas kernels for 0%

profile of v1, /device:TPU:3, one launch (start us, length us, event | category | flops | bytes accessed | tf_op | source)
XLA Modules:
  0.0 320.0 jit_solution(2556117927788334304)
XLA Ops:
  7.3 2.1 fusion.64
  9.4 3.2 collective-permute-start
  12.6 2.9 collective-permute-start.1
  15.5 22.7 %collective-permute-done = bf16[9,1,120,256]{3,2,1,0:T(8,128)(2,1)} collective-permute-done((bf16[9,1,120,256]{3,2,1,0:T(8,128)(2,1)S(1)}, bf16[9,1,120,256]{3,2,1,0:T(8,128)(2,1)}, u32[]{:S(2)}, u32[]{:S(2)}) %collective-permute-start) | collective-permute-done | bytes 552992 | tf_op jit(solution)/shard_map/ppermute | solution.py:18
  38.2 1.1 constant_dynamic-update-slice_fusion.2
  39.3 1.8 constant_dynamic-update-slice_fusion.1
  41.1 1.1 constant_dynamic-update-slice_fusion
  42.3 4.6 %collective-permute-start.2 = (bf16[9,6,1,256]{3,2,1,0:T(2,128)(2,1)S(1)}, bf16[9,6,1,256]{3,2,1,0:T(2,128)(2,1)S(1)}, u32[]{:S(2)}, u32[]{:S(2)}) collective-permute-start(bf16[9,6,1,256]{3,2,1,0:T(2,128)(2,1)S(1)} %get-tuple-element.6), channel_id=1, source_target_pairs={{0,1},{1,2},{2,3},{4,5},{5,6},{6,7},{8,9},{9,10},{10,11},{12,13},{... | collective-permute-start | bytes 82952 | tf_op jit(solution)/shard_map/ppermute | solution.py:18
  46.9 25.9 %all_gather.16 = bf16[256,768]{1,0:T(8,128)(2,1)} all-gather(bf16[32,768]{1,0:T(8,128)(2,1)S(1)} %copy-done.12), channel_id=1, replica_groups=mesh['rows'=8,'chan'=4] {'rows'}, dimensions={0}, use_global_device_ids=true | all-gather | bytes 442368 | tf_op jit(solution)/shard_map/all_gather | solution.py:110
  72.8 5.5 %collective-permute-start.3 = (bf16[9,6,1,256]{3,2,1,0:T(2,128)(2,1)S(1)}, bf16[9,6,1,256]{3,2,1,0:T(2,128)(2,1)S(1)}, u32[]{:S(2)}, u32[]{:S(2)}) collective-permute-start(bf16[9,6,1,256]{3,2,1,0:T(2,128)(2,1)S(1)} %get-tuple-element.5), channel_id=1, source_target_pairs={{1,0},{2,1},{3,2},{5,4},{6,5},{7,6},{9,8},{10,9},{11,10},{13,12},{... | collective-permute-start | bytes 82952 | tf_op jit(solution)/shard_map/ppermute | solution.py:20
  78.4 3.8 %fusion.15 = f32[9,4,120,256]{3,2,1,0:T(8,128)} fusion(bf16[9,6,120,256]{3,2,1,0:T(8,128)(2,1)S(1)} %constant_dynamic-update-slice_fusion, bf16[9,6,1,256]{3,2,1,0:T(2,128)(2,1)S(1)} %collective-permute-done.2, bf16[256,2304]{1,0:T(8,128)(2,1)} %all-gather.5.cloned.1.call-done), kind=kOutput, calls=%fused_computation.29 | convolution fusion | flops 570654720 | bytes 7900160 | tf_op jit(solution)/shard_map/fijc,co->fijo/dot_general | solution.py:44
  82.2 2.8 fusion.18
  85.0 2.8 fusion.12
  87.8 2.9 fusion.9
  90.7 2.9 fusion.22
  93.6 3.9 %fusion = f32[9,4,120,256]{3,2,1,0:T(8,128)} fusion(bf16[9,4,120,256]{3,2,1,0:T(8,128)(2,1)S(1)} %copy-done, bf16[9,1,120,256]{3,2,1,0:T(8,128)(2,1)} %collective-permute-done, bf16[256,2304]{1,0:T(8,128)(2,1)S(1)} %copy-done.11), kind=kOutput, calls=%fused_computation.15 | convolution fusion | flops 571760640 | bytes 7319552 | tf_op jit(solution)/shard_map/fijc,co->fijo/dot_general | solution.py:44
  97.4 1.8 fusion.4
  99.2 2.9 fusion.50
  102.1 12.6 %add_convert_fusion = bf16[9,4,120,256]{3,2,1,0:T(8,128)(2,1)} fusion(f32[9,4,120,256]{3,2,1,0:T(8,128)S(1)} %fusion.4, f32[9,4,120,256]{3,2,1,0:T(8,128)} %fusion.22, f32[9,4,120,256]{3,2,1,0:T(8,128)} %fusion.9, f32[9,4,120,256]{3,2,1,0:T(8,128)} %fusion.50, f32[9,4,120,256]{3,2,1,0:T(8,128)} %fusion.15, f32[9,4,120,256]{3,2,1,0:T(8,128)} %fusion.12, ...), kind=kOutput, calls=%fused_computation.7 | convolution fusion | flops 580608000 | bytes 41105408 | tf_op jit(solution)/shard_map/fijc,co->fijo/dot_general | solution.py:44
  114.7 1.6 copy-done.1
  120.3 3.0 fusion.65
  123.8 38.8 %all-reduce = f32[1024]{0:T(1024)S(1)} all-reduce(f32[1024]{0:T(1024)S(1)} %dynamic-update-slice), channel_id=2, replica_groups=mesh['rows'=8,'chan'=4] {'rows','chan'}, use_global_device_ids=true, to_apply=%add | all-reduce | flops 1024 | bytes 8192
  162.8 2.9 multiply_reduce_fusion
  166.1 41.6 %all-reduce.1 = f32[1024]{0:T(1024)S(1)} all-reduce(f32[1024]{0:T(1024)S(1)} %dynamic-update-slice.1), channel_id=3, replica_groups=mesh['rows'=8,'chan'=4] {'rows','chan'}, use_global_device_ids=true, to_apply=%add.1 | all-reduce | flops 1024 | bytes 8192
  208.1 3.6 %multiply_convert_fusion = bf16[9,4,120,256]{3,2,1,0:T(8,128)(2,1)S(1)} fusion(f32[9,4,120,256]{3,2,1,0:T(8,128)} %get-tuple-element.12, f32[256]{0:T(256)S(1)} %copy-done.13, f32[256]{0:T(256)S(1)} %copy-done.14, f32[256]{0:T(256)S(1)} %rsqrt.12, f32[256]{0:T(256)S(1)} %sub.10), kind=kLoop, calls=%fused_computation.4 | loop fusion | flops 9953280 | bytes 6639616 | tf_op jit(solution)/shard_map/convert_element_type | solution.py:132
  212.6 1.9 collective-permute-start.4
  215.4 2.2 fusion.48
  217.6 10.4 %collective-permute-done.4 = bf16[9,1,120,256]{3,2,1,0:T(8,128)(2,1)S(1)} collective-permute-done((bf16[9,1,120,256]{3,2,1,0:T(8,128)(2,1)}, bf16[9,1,120,256]{3,2,1,0:T(8,128)(2,1)S(1)}, u32[]{:S(2)}, u32[]{:S(2)}) %collective-permute-start.4) | collective-permute-done | bytes 552992 | tf_op jit(solution)/shard_map/ppermute | solution.py:30
  228.0 1.8 pad_maximum_fusion
  229.8 10.3 %slice.188 = bf16[9,2,60,256]{3,2,1,0:T(8,128)(2,1)} slice(bf16[9,5,120,256]{3,2,1,0:T(8,128)(2,1)} %pad_maximum_fusion), slice={[0:9:1], [1:5:2], [0:120:2], [0:256:1]} | slice | bytes 1105920 | tf_op jit(solution)/shard_map/slice | solution.py:78
  240.1 8.5 %slice.194 = bf16[9,2,60,256]{3,2,1,0:T(8,128)(2,1)S(1)} slice(bf16[9,5,120,256]{3,2,1,0:T(8,128)(2,1)} %pad_maximum_fusion), slice={[0:9:1], [2:5:2], [0:120:2], [0:256:1]} | slice | bytes 1105920 | tf_op jit(solution)/shard_map/slice | solution.py:78
  248.7 4.5 %collective-permute-start.5 = (bf16[9,5,1,256]{3,2,1,0:T(2,128)(2,1)S(1)}, bf16[9,5,1,256]{3,2,1,0:T(2,128)(2,1)S(1)}, u32[]{:S(2)}, u32[]{:S(2)}) collective-permute-start(bf16[9,5,1,256]{3,2,1,0:T(2,128)(2,1)S(1)} %fusion.51), channel_id=1, source_target_pairs={{1,0},{2,1},{3,2},{5,4},{6,5},{7,6},{9,8},{10,9},{11,10},{13,12},{... | collective-permute-start | bytes 69128 | tf_op jit(solution)/shard_map/ppermute | solution.py:30
  253.2 2.3 fusion.47
  255.5 2.2 fusion.44
  257.7 2.0 pad_maximum_fusion.1
  259.7 10.5 %slice.184 = bf16[9,2,60,256]{3,2,1,0:T(8,128)(2,1)} slice(bf16[9,5,121,256]{3,2,1,0:T(8,128)(2,1)} %pad_maximum_fusion.1), slice={[0:9:1], [0:4:2], [1:121:2], [0:256:1]} | slice | bytes 1105920 | tf_op jit(solution)/shard_map/slice | solution.py:78
  270.2 10.1 %slice.198 = bf16[9,2,60,256]{3,2,1,0:T(8,128)(2,1)} slice(bf16[9,5,121,256]{3,2,1,0:T(8,128)(2,1)} %pad_maximum_fusion.1), slice={[0:9:1], [2:5:2], [2:121:2], [0:256:1]} | slice | bytes 1105920 | tf_op jit(solution)/shard_map/slice | solution.py:78
  280.3 10.1 %slice.196 = bf16[9,2,60,256]{3,2,1,0:T(8,128)(2,1)} slice(bf16[9,5,121,256]{3,2,1,0:T(8,128)(2,1)} %pad_maximum_fusion.1), slice={[0:9:1], [2:5:2], [1:121:2], [0:256:1]} | slice | bytes 1105920 | tf_op jit(solution)/shard_map/slice | solution.py:78
  290.4 6.0 %slice.192 = bf16[9,2,60,256]{3,2,1,0:T(8,128)(2,1)} slice(bf16[9,5,121,256]{3,2,1,0:T(8,128)(2,1)S(1)} %copy-done.2), slice={[0:9:1], [1:5:2], [2:121:2], [0:256:1]} | slice | bytes 1105920 | tf_op jit(solution)/shard_map/slice | solution.py:78
  296.4 5.9 %slice.190 = bf16[9,2,60,256]{3,2,1,0:T(8,128)(2,1)} slice(bf16[9,5,121,256]{3,2,1,0:T(8,128)(2,1)S(1)} %copy-done.2), slice={[0:9:1], [1:5:2], [1:121:2], [0:256:1]} | slice | bytes 1105920 | tf_op jit(solution)/shard_map/slice | solution.py:78
  302.3 1.0 slice.186
  303.4 1.5 fusion.42
  304.9 1.5 fusion.43
  306.4 1.2 fusion.45
  307.7 1.4 fusion.46
  309.0 1.2 convolution_add_fusion.1
  310.3 1.5 fusion.41
  311.8 1.4 copy.10
  (71 shorter events, 8.1 us)
Async XLA Ops:
  6.5 71.8 %all-gather.5.cloned.1.call-start = ((), (), s32[]{:S(2)}) async-start(), calls=%async_computation | async-start | bytes 1327104 | tf_op jit(solution)/shard_map/all_gather | solution.py:109
  7.3 208.1 %all-gather.7.cloned.1.call-start = ((), (), s32[]{:S(2)}) async-start(), calls=%async_computation.1 | async-start | bytes 1327104 | tf_op jit(solution)/shard_map/all_gather | solution.py:111
  9.4 28.8 %collective-permute-start = (bf16[9,1,120,256]{3,2,1,0:T(8,128)(2,1)S(1)}, bf16[9,1,120,256]{3,2,1,0:T(8,128)(2,1)}, u32[]{:S(2)}, u32[]{:S(2)}) collective-permute-start(bf16[9,1,120,256]{3,2,1,0:T(8,128)(2,1)S(1)} %get-tuple-element.9), channel_id=1, source_target_pairs={{0,4},{4,8},{8,12},{12,16},{16,20},{20,24},{24,28},{1,5},{5,9},{9,... | collective-permute-start | bytes 1658888 | tf_op jit(solution)/shard_map/ppermute | solution.py:18
  12.6 28.5 %collective-permute-start.1 = (bf16[9,1,120,256]{3,2,1,0:T(8,128)(2,1)}, bf16[9,1,120,256]{3,2,1,0:T(8,128)(2,1)}, u32[]{:S(2)}, u32[]{:S(2)}) collective-permute-start(bf16[9,1,120,256]{3,2,1,0:T(8,128)(2,1)} %get-tuple-element.10), channel_id=1, source_target_pairs={{4,0},{8,4},{12,8},{16,12},{20,16},{24,20},{28,24},{5,1},{9,5},{13... | collective-permute-start | bytes 1658888 | tf_op jit(solution)/shard_map/ppermute | solution.py:20
  39.3 7.6 %copy-start.12 = (bf16[32,768]{1,0:T(8,128)(2,1)S(1)}, bf16[32,768]{1,0:T(8,128)(2,1)}, u32[]{:S(2)}) copy-start(bf16[32,768]{1,0:T(8,128)(2,1)} %param.9) | copy-start | bytes 147460
  42.3 36.0 %collective-permute-start.2 = (bf16[9,6,1,256]{3,2,1,0:T(2,128)(2,1)S(1)}, bf16[9,6,1,256]{3,2,1,0:T(2,128)(2,1)S(1)}, u32[]{:S(2)}, u32[]{:S(2)}) collective-permute-start(bf16[9,6,1,256]{3,2,1,0:T(2,128)(2,1)S(1)} %get-tuple-element.6), channel_id=1, source_target_pairs={{0,1},{1,2},{2,3},{4,5},{5,6},{6,7},{8,9},{9,10},{10,11},{12,13},{... | collective-permute-start | bytes 82952 | tf_op jit(solution)/shard_map/ppermute | solution.py:18
  72.8 12.2 %collective-permute-start.3 = (bf16[9,6,1,256]{3,2,1,0:T(2,128)(2,1)S(1)}, bf16[9,6,1,256]{3,2,1,0:T(2,128)(2,1)S(1)}, u32[]{:S(2)}, u32[]{:S(2)}) collective-permute-start(bf16[9,6,1,256]{3,2,1,0:T(2,128)(2,1)S(1)} %get-tuple-element.5), channel_id=1, source_target_pairs={{1,0},{2,1},{3,2},{5,4},{6,5},{7,6},{9,8},{10,9},{11,10},{13,12},{... | collective-permute-start | bytes 82952 | tf_op jit(solution)/shard_map/ppermute | solution.py:20
  78.4 3.8 %copy-start.11 = (bf16[256,2304]{1,0:T(8,128)(2,1)S(1)}, bf16[256,2304]{1,0:T(8,128)(2,1)}, u32[]{:S(2)}) copy-start(bf16[256,2304]{1,0:T(8,128)(2,1)} %all-gather.5.cloned.1.call-done) | copy-start | bytes 3538948
  90.7 2.9 copy-start
  114.7 1.6 copy-start.1
  116.3 1.0 copy-start.10
  117.3 1.5 slice-start
  118.8 1.5 slice-start.1
  123.3 84.7 %copy-start.13 = (f32[256]{0:T(256)S(1)}, f32[256]{0:T(256)}, u32[]{:S(2)}) copy-start(f32[256]{0:T(256)} %param.12) | copy-start | bytes 3076
  123.3 84.7 %copy-start.14 = (f32[256]{0:T(256)S(1)}, f32[256]{0:T(256)}, u32[]{:S(2)}) copy-start(f32[256]{0:T(256)} %param.11) | copy-start | bytes 3076
  212.6 15.5 %collective-permute-start.4 = (bf16[9,1,120,256]{3,2,1,0:T(8,128)(2,1)}, bf16[9,1,120,256]{3,2,1,0:T(8,128)(2,1)S(1)}, u32[]{:S(2)}, u32[]{:S(2)}) collective-permute-start(bf16[9,1,120,256]{3,2,1,0:T(8,128)(2,1)} %slice.226), channel_id=1, source_target_pairs={{4,0},{8,4},{12,8},{16,12},{20,16},{24,20},{28,24},{5,1},{9,5},{13... | collective-permute-start | bytes 1658888 | tf_op jit(solution)/shard_map/ppermute | solution.py:30
  248.6 4.6 %copy-start.8 = (bf16[9,2,60,256]{3,2,1,0:T(8,128)(2,1)S(1)}, bf16[9,2,60,256]{3,2,1,0:T(8,128)(2,1)}, u32[]{:S(2)}) copy-start(bf16[9,2,60,256]{3,2,1,0:T(8,128)(2,1)} %slice.188) | copy-start | bytes 1658884
  248.7 9.0 %collective-permute-start.5 = (bf16[9,5,1,256]{3,2,1,0:T(2,128)(2,1)S(1)}, bf16[9,5,1,256]{3,2,1,0:T(2,128)(2,1)S(1)}, u32[]{:S(2)}, u32[]{:S(2)}) collective-permute-start(bf16[9,5,1,256]{3,2,1,0:T(2,128)(2,1)S(1)} %fusion.51), channel_id=1, source_target_pairs={{1,0},{2,1},{3,2},{5,4},{6,5},{7,6},{9,8},{10,9},{11,10},{13,12},{... | collective-permute-start | bytes 69128 | tf_op jit(solution)/shard_map/ppermute | solution.py:30
  259.7 30.7 %copy-start.2 = (bf16[9,5,121,256]{3,2,1,0:T(8,128)(2,1)S(1)}, bf16[9,5,121,256]{3,2,1,0:T(8,128)(2,1)}, u32[]{:S(2)}) copy-start(bf16[9,5,121,256]{3,2,1,0:T(8,128)(2,1)} %pad_maximum_fusion.1) | copy-start | bytes 8363524
  303.3 3.1 copy-start.9
  303.3 4.3 %copy-start.7 = (bf16[9,2,60,256]{3,2,1,0:T(8,128)(2,1)S(1)}, bf16[9,2,60,256]{3,2,1,0:T(8,128)(2,1)}, u32[]{:S(2)}) copy-start(bf16[9,2,60,256]{3,2,1,0:T(8,128)(2,1)} %slice.190) | copy-start | bytes 1658884
  304.8 4.2 %copy-start.5 = (f32[9,2,60,256]{3,2,1,0:T(8,128)S(1)}, f32[9,2,60,256]{3,2,1,0:T(8,128)}, u32[]{:S(2)}) copy-start(f32[9,2,60,256]{3,2,1,0:T(8,128)} %fusion.48) | copy-start | bytes 3317764
  304.9 4.2 %copy-start.6 = (bf16[9,2,60,256]{3,2,1,0:T(8,128)(2,1)S(1)}, bf16[9,2,60,256]{3,2,1,0:T(8,128)(2,1)}, u32[]{:S(2)}) copy-start(bf16[9,2,60,256]{3,2,1,0:T(8,128)(2,1)} %slice.184) | copy-start | bytes 1658884
  307.6 2.6 copy-start.3
  307.6 2.6 copy-start.4
  307.6 2.6 copy-start.15
Sparse Core Ops, SparseCore 0:
  9.5 52.3 all-gather.4
  64.2 39.7 all-gather.6
